TPU v7x, 512 devices: a whole 4x4x16 slice. The times are simulated.
512 devices in a mesh: grid: 64 (over y_lo, z, core), dp: 8 (over y_hi, x).
Axes of the slice: x: 4, y: 4 (y_hi: 2, y_lo: 2; y = y_hi * 2 + y_lo), z: 16, core: 2. Of those that a mesh axis runs over, the one named last changes fastest.
Arguments:
- field: bfloat16 [65536, 1024], P('grid', 'dp'), may hold values from -6 to 6
- cotangent: bfloat16 [65536, 1024], P('grid', 'dp'), may hold values from -6 to 6
- mode_blocks: int32 [8], replicated, may hold values from 0 to 4095, as said below
- spectral: bfloat16 [2, 64, 64, 64], P(None, 'grid'), may hold values from -6 to 6
- w_in: bfloat16 [64, 256], replicated, may hold values from -0.75 to 0.75
- b_in: float32 [256], replicated, may hold values from -3 to 3
- w_out: bfloat16 [256, 64], replicated, may hold values from -0.375 to 0.375
- b_out: float32 [64], replicated, may hold values from -3 to 3
Outputs:
- output: bfloat16 [65536, 1024], P('grid', 'dp')
- field_grad: bfloat16 [65536, 1024], P('grid', 'dp')
- spectral_grad: float32 [2, 64, 64, 64], P(None, 'grid')
- w_in_grad: float32 [64, 256], replicated
- b_in_grad: float32 [256], replicated
- w_out_grad: float32 [256, 64], replicated
- b_out_grad: float32 [64], replicated
Inputs may be any that keep to these rules, and one draw needn't show every extreme that they name: `mode_blocks`: distinct block numbers; 0 and 4095 are always among them.
All inputs are finite; a program needn't handle non-finite values.
Results may differ from a plain program's by a relative error of at most 0.013.
Values may be sent and summed in bfloat16 or wider, within the bound.
No kernel may reach another device: no remote copies, remote signals or barrier semaphores. Data moves between devices by JAX's collectives and lax.ppermute only.
A program may use at most 64 MiB of HBM per device.

v0:
```python
import math
import jax
import jax.numpy as jnp
from jax import lax
from jax.sharding import PartitionSpec as P

NX = 65536
BLK = 8


def mode_list(mode_blocks, block_width):
    offsets = jnp.arange(block_width, dtype=jnp.int32)
    return (mode_blocks[:, None] * block_width + offsets[None, :]).reshape(-1)


def forward_table(modes, first_row, count, length):
    rows_here = first_row + jnp.arange(count, dtype=jnp.int32)
    product = modes[:, None] * rows_here[None, :] % length
    phase = product.astype(jnp.float32) * (2.0 * math.pi / length)
    scale = 1.0 / math.sqrt(length)
    table = jnp.stack([jnp.cos(phase) * scale, -jnp.sin(phase) * scale], axis=1)
    return table.reshape(2 * modes.shape[0], count).astype(jnp.bfloat16)


def inverse_table(forward):
    return (forward.astype(jnp.float32) * 2.0).astype(jnp.bfloat16).T


def gelu_grad(pre):
    _, pull = jax.vjp(jax.nn.gelu, pre)
    return pull(jnp.ones_like(pre))[0]


def mix(real, imag, weight_re, weight_im):
    best = lax.Precision.HIGHEST
    out_re = jnp.einsum("kbi,kio->kbo", real, weight_re, precision=best) - jnp.einsum(
        "kbi,kio->kbo", imag, weight_im, precision=best
    )
    out_im = jnp.einsum("kbi,kio->kbo", real, weight_im, precision=best) + jnp.einsum(
        "kbi,kio->kbo", imag, weight_re, precision=best
    )
    return (out_re, out_im)


def mix_grads(real, imag, grad_re, grad_im, weight_re, weight_im):
    best = lax.Precision.HIGHEST
    w_re = jnp.einsum("kbi,kbo->kio", real, grad_re, precision=best) + jnp.einsum(
        "kbi,kbo->kio", imag, grad_im, precision=best
    )
    w_im = jnp.einsum("kbi,kbo->kio", real, grad_im, precision=best) - jnp.einsum(
        "kbi,kbo->kio", imag, grad_re, precision=best
    )
    in_re = jnp.einsum("kbo,kio->kbi", grad_re, weight_re, precision=best) + jnp.einsum(
        "kbo,kio->kbi", grad_im, weight_im, precision=best
    )
    in_im = jnp.einsum("kbo,kio->kbi", grad_im, weight_re, precision=best) - jnp.einsum(
        "kbo,kio->kbi", grad_re, weight_im, precision=best
    )
    return (w_re, w_im, in_re, in_im)


def pointwise_pass(field, spec, cotangent, w_in, b_in, w_out, b_out):
    chans = w_in.shape[0]
    shape = field.shape
    spec_rows = spec.reshape(-1, chans)
    pre = jnp.dot(spec_rows, w_in, preferred_element_type=jnp.float32) + b_in
    hidden = jax.nn.gelu(pre).astype(jnp.bfloat16)
    out = jnp.dot(hidden, w_out, preferred_element_type=jnp.float32) + b_out
    result = (
        (field.reshape(-1, chans).astype(jnp.float32) + out).astype(jnp.bfloat16).reshape(shape)
    )
    upstream = cotangent.reshape(-1, chans)
    grad_w_out = jnp.einsum("nh,nc->hc", hidden, upstream, preferred_element_type=jnp.float32)
    grad_b_out = jnp.sum(upstream.astype(jnp.float32), axis=0)
    grad_hidden = jnp.einsum("nc,hc->nh", upstream, w_out, preferred_element_type=jnp.float32)
    grad_pre = (grad_hidden * gelu_grad(pre)).astype(jnp.bfloat16)
    grad_w_in = jnp.einsum("nc,nh->ch", spec_rows, grad_pre, preferred_element_type=jnp.float32)
    grad_b_in = jnp.sum(grad_pre.astype(jnp.float32), axis=0)
    grad_spec = (
        jnp.einsum("nh,ch->nc", grad_pre, w_in, preferred_element_type=jnp.float32)
        .astype(jnp.bfloat16)
        .reshape(shape)
    )
    return (result, grad_spec, (grad_w_in, grad_b_in, grad_w_out, grad_b_out))


def local(field, cotangent, mode_blocks, spectral, w_in, b_in, w_out, b_out):
    rows = field.shape[0]
    width = field.shape[1]
    chans = w_in.shape[0]
    ncol = width // chans
    own = spectral.shape[1]
    modes = mode_list(mode_blocks, BLK)
    columns_total = ncol * lax.axis_size("dp")
    first = lax.axis_index("grid") * rows
    forward_here = forward_table(modes, first, rows, NX)
    inverse_here = inverse_table(forward_here)
    weight_re = spectral[0].astype(jnp.float32)
    weight_im = spectral[1].astype(jnp.float32)
    part = forward_here
    modal = lax.psum_scatter(
        jnp.dot(part, field, preferred_element_type=jnp.float32).reshape(
            own * lax.axis_size("grid"), 2 * width
        ),
        "grid",
        scatter_dimension=0,
        tiled=True,
    ).reshape(own, 2, ncol, chans)
    real = modal[:, 0]
    imag = modal[:, 1]
    out_re, out_im = mix(real, imag, weight_re, weight_im)
    mixed = jnp.stack([out_re, out_im], axis=1).reshape(own, 2 * width).astype(jnp.bfloat16)
    piece = lax.all_gather(mixed, "grid", axis=0, tiled=True)
    count = piece.shape[0]
    part = inverse_here
    spec = jnp.dot(
        part, piece.reshape(2 * count, width), preferred_element_type=jnp.float32
    ).astype(jnp.bfloat16)
    output, grad_spec, sums = pointwise_pass(field, spec, cotangent, w_in, b_in, w_out, b_out)
    part = inverse_here
    grad_modal = lax.psum_scatter(
        jnp.einsum("rm,rw->mw", part, grad_spec, preferred_element_type=jnp.float32).reshape(
            own * lax.axis_size("grid"), 2 * width
        ),
        "grid",
        scatter_dimension=0,
        tiled=True,
    ).reshape(own, 2, ncol, chans)
    w_re, w_im, in_re, in_im = mix_grads(
        real, imag, grad_modal[:, 0], grad_modal[:, 1], weight_re, weight_im
    )
    grad_in = jnp.stack([in_re, in_im], axis=1).reshape(own, 2 * width).astype(jnp.bfloat16)
    piece = lax.all_gather(grad_in, "grid", axis=0, tiled=True)
    count = piece.shape[0]
    part = forward_here
    back = jnp.einsum(
        "mr,mw->rw", part, piece.reshape(2 * count, width), preferred_element_type=jnp.float32
    )
    field_grad = (cotangent.astype(jnp.float32) + back).astype(jnp.bfloat16)
    spectral_part = jnp.stack([w_re, w_im], axis=0)
    spectral_sum = lax.psum(spectral_part.astype(jnp.bfloat16), "dp").astype(jnp.float32)
    grad_w_in, grad_b_in, grad_w_out, grad_b_out = lax.psum(
        (sums[0], sums[1], sums[2], sums[3]), ("grid", "dp")
    )
    inv_cols = 1.0 / columns_total
    return (
        output,
        field_grad,
        spectral_sum * inv_cols,
        grad_w_in * inv_cols,
        grad_b_in * inv_cols,
        grad_w_out * inv_cols,
        grad_b_out * inv_cols,
    )


def solution(mesh):
    in_specs = (
        P("grid", "dp"),
        P("grid", "dp"),
        P(),
        P(None, "grid", None, None),
        P(),
        P(),
        P(),
        P(),
    )
    out_specs = (P("grid", "dp"), P("grid", "dp"), P(None, "grid", None, None), P(), P(), P(), P())
    return jax.shard_map(local, mesh=mesh, in_specs=in_specs, out_specs=out_specs, check_vma=False)
```

profile of v0, /device:TPU:1, one launch (start us, length us, event | category | flops | bytes accessed | tf_op | source)
XLA Modules:
  0.0 1456.2 jit_solution(12951280648803934894)
XLA Ops:
  7.3 0.7 broadcast_multiply_fusion.4
  8.0 0.1 iota_add_fusion.1
  8.0 0.1 add.107
  8.1 1.2 cosine_multiply_fusion
  9.4 0.3 copy.27
  9.7 0.1 convert_element_type.146
  9.8 0.2 fusion.47
  10.0 0.6 reshape.368
  10.7 0.0 all-reduce.12.cloned.1.call-start
  10.8 0.2 reshape.377
  11.0 0.3 convert_reduce_fusion.1
  11.3 0.2 reshape.384
  11.5 0.3 copy.26
  11.8 0.1 convert_element_type.145
  11.9 0.3 copy.28
  12.2 1.3 dynamic-slice
  13.5 363.8 %all-reduce.8.cloned.1.call-done = f32[64,256]{1,0:T(8,128)} async-done(((f32[64,256]{1,0:T(8,128)}), f32[64,256]{1,0:T(8,128)}) %all-reduce.8.cloned.1.call-update) | async-done | bytes 65552
  377.3 1.4 dynamic-slice_reduce_fusion.1
  378.7 0.1 reshape.369
  378.8 0.1 fusion.27
  378.9 0.1 fusion.35
  379.0 0.1 fusion.20
  379.1 0.1 fusion.21
  379.3 0.1 reshape.385
  379.4 61.0 %all-gather = bf16[64,1,256]{2,1,0:T(2,128)(2,1)S(1)} all-gather(bf16[1,1,256]{2,1,0:T(2,128)(2,1)S(1)} %reshape.385), channel_id=1, replica_groups=mesh['grid'=64,'dp'=8] {'grid'}, dimensions={0}, use_global_device_ids=true | all-gather | bytes 33280 | tf_op jit(solution)/shard_map/all_gather | solution.py:113
  440.3 0.2 reduce.1
  440.5 0.3 convolution_convert_fusion.1
  440.8 0.2 reshape.375
  441.1 0.9 multiply_convert_fusion
  442.0 1.5 convert_reduce_fusion
  443.5 0.9 fusion.49
  444.4 0.4 convolution_convert_fusion
  444.9 0.9 fusion.50
  445.8 0.3 copy.30
  446.1 0.3 reshape.378
  446.4 0.2 fusion.48
  446.6 101.6 %all-reduce.2 = (f32[256]{0:T(256)S(1)}, f32[64]{0:T(128)S(1)}) all-reduce(f32[256]{0:T(256)S(1)} %get-tuple-element.17, f32[64]{0:T(128)S(1)} %convert_reduce_fusion.1), channel_id=1, replica_groups=mesh['grid'=64,'dp'=8] {'grid','dp'}, use_global_device_ids=true, to_apply=%region_5.6 | all-reduce | flops 320 | bytes 2560 | tf_op jit(solution)/shard_map/psum | solution.py:142
  548.2 0.6 broadcast_multiply_fusion.2
  548.8 0.0 all-reduce.10.cloned.1.call-start
  548.8 0.4 fusion.2
  549.3 0.5 broadcast_multiply_fusion.3
  549.8 0.6 reshape.379
  550.5 0.3 copy.29
  550.7 1.0 reshape.376
  551.7 437.2 %all-reduce.12.cloned.1.call-done = (f32[64,256]{1,0:T(8,128)}, f32[256,64]{0,1:T(8,128)}) async-done(((f32[64,256]{1,0:T(8,128)}, f32[256,64]{0,1:T(8,128)}), (f32[64,256]{1,0:T(8,128)}, f32[256,64]{0,1:T(8,128)})) %all-reduce.12.cloned.1.call-update) | async-done | bytes 131088 | tf_op jit(solution)/shard_map/psum | solution.py:142
  988.9 1.5 broadcast_multiply_fusion
  990.4 1.5 broadcast_multiply_fusion.1
  991.9 351.2 %all-reduce.10.cloned.1.call-done = f32[64,256]{1,0:T(8,128)} async-done(((f32[64,256]{1,0:T(8,128)}), f32[64,256]{1,0:T(8,128)}) %all-reduce.10.cloned.1.call-update) | async-done | bytes 65552
  1343.1 1.4 dynamic-slice_reduce_fusion
  1344.5 0.1 reshape.380
  1344.5 0.2 fusion.46
  1344.8 0.2 fusion.45
  1345.0 0.1 fusion.32
  1345.1 0.1 fusion.30
  1345.3 0.3 fusion.13
  1345.6 0.2 fusion.12
  1345.8 34.1 %psum.35 = bf16[2,1,64,64]{3,2,1,0:T(8,128)(2,1)S(1)} all-reduce(bf16[2,1,64,64]{3,2,1,0:T(8,128)(2,1)S(1)} %pad_maximum_fusion), channel_id=1, replica_groups=mesh['grid'=64,'dp'=8] {'dp'}, use_global_device_ids=true, to_apply=%region_2.3 | all-reduce | flops 8192 | bytes 32768 | tf_op jit(solution)/shard_map/psum | solution.py:141
  1380.0 0.6 convert_multiply_fusion
  1380.6 0.1 fusion.19
  1380.7 0.1 fusion.18
  1380.9 0.1 reshape.387
  1381.0 67.5 %all-gather.1 = bf16[64,1,256]{2,1,0:T(2,128)(2,1)S(1)} all-gather(bf16[1,1,256]{2,1,0:T(2,128)(2,1)S(1)} %reshape.387), channel_id=1, replica_groups=mesh['grid'=64,'dp'=8] {'grid'}, dimensions={0}, use_global_device_ids=true | all-gather | bytes 33280 | tf_op jit(solution)/shard_map/all_gather | solution.py:133
  1448.5 0.2 reduce.3
  1448.7 1.0 fusion.9
  (25 shorter events, 0.3 us)
Async XLA Ops:
  7.2 433.9 %copy-start = (bf16[64,256]{1,0:T(8,128)(2,1)S(1)}, bf16[64,256]{1,0:T(8,128)(2,1)}, u32[]{:S(2)}) copy-start(bf16[64,256]{1,0:T(8,128)(2,1)} %param.12) | copy-start | bytes 98308
  7.2 2.6 copy-start.2
  7.2 3.6 copy-start.1
  7.2 370.1 %all-reduce.8.cloned.1.call-start = ((), (), s32[]{:S(2)}) async-start(), calls=%async_computation | async-start | bytes 131072
  10.7 978.2 %all-reduce.12.cloned.1.call-start = ((), (), s32[]{:S(2)}) async-start(), calls=%async_computation.2 | async-start | bytes 262144 | tf_op jit(solution)/shard_map/psum | solution.py:142
  11.3 367.4 %copy-start.3 = (bf16[2,1,64,64]{3,2,1,0:T(8,128)(2,1)S(1)}, bf16[2,1,64,64]{3,2,1,0:T(8,128)(2,1)}, u32[]{:S(2)}) copy-start(bf16[2,1,64,64]{3,2,1,0:T(8,128)(2,1)} %param.11) | copy-start | bytes 49156
  11.5 429.6 %copy-start.6 = (f32[256]{0:T(256)S(1)}, f32[256]{0:T(256)}, u32[]{:S(2)}) copy-start(f32[256]{0:T(256)} %param.13) | copy-start | bytes 3076
  441.1 0.9 copy-start.4
  444.9 104.0 %copy-start.5 = (f32[64]{0:T(128)S(1)}, f32[64]{0:T(128)}, u32[]{:S(2)}) copy-start(f32[64]{0:T(128)} %param.15) | copy-start | bytes 772
  548.8 794.3 %all-reduce.10.cloned.1.call-start = ((), (), s32[]{:S(2)}) async-start(), calls=%async_computation.1 | async-start | bytes 131072
Sparse Core Ops, SparseCore 0:
  11.5 365.7 all-reduce.7
  548.9 439.9 all-reduce.11
  992.4 350.6 all-reduce.9
where the time goes:
time: 1460 us
  waiting for transfers between devices  1150 us (79%)
  blocking collectives  264 us (18%)
    unnamed x5, waiting for transfers between devices  715 us
    psum x1, waiting for transfers between devices, local(): lax.psum((sums[0], sums[1], sums[2], sums[3]), ('grid', 'dp'))  437 us
    psum x1, blocking collectives, local(): lax.psum((sums[0], sums[1], sums[2], sums[3]), ('grid', 'dp'))  102 us
    all_gather x1, blocking collectives, local(): piece = lax.all_gather(grad_in, 'grid', axis=0, tiled=True)  67.5 us
    all_gather x1, blocking collectives, local(): piece = lax.all_gather(mixed, 'grid', axis=0, tiled=True)  61 us
    psum x1, blocking collectives, local(): lax.psum(spectral_part.astype(jnp.bfloat16), 'dp').astype(jnp.float32)  34.1 us
  transfers between devices with their start and end apart: 3, of which 3 were waited for; matrix products, arithmetic and copies ran while one was open for 1% of the time, Pallas kernels for 0%

commit v1 on v0

--- a/solution.py
+++ b/solution.py
@@ -140,7 +140,7 @@
     spectral_part = jnp.stack([w_re, w_im], axis=0)
     spectral_sum = lax.psum(spectral_part.astype(jnp.bfloat16), "dp").astype(jnp.float32)
     grad_w_in, grad_b_in, grad_w_out, grad_b_out = lax.psum(
-        (sums[0], sums[1], sums[2], sums[3]), ("grid", "dp")
+        lax.psum((sums[0], sums[1], sums[2], sums[3]), "dp"), "grid"
     )
     inv_cols = 1.0 / columns_total
     return (

time: 1460 us -> 1160 us (0.79)
  waiting for transfers between devices: 1150 us -> 830 us
  blocking collectives: 264 us -> 291 us
    psum x1, waiting for transfers between devices: 437 us -> 80.8 us  [local(): lax.psum((sums[0], sums[1], sums[2], sums[3]), 'dp')]
    unnamed x5, waiting for transfers between devices: 715 us -> 749 us
    psum x1 -> x2, blocking collectives: 102 us -> 127 us  [the longest x1 108 us: local(): lax.psum(lax.psum((sums[0], sums[1], sums[2], sums[3]), 'dp'), 'grid')]
  transfers between devices with their start and end apart: 3 -> 3, of which waited for: 3 -> 3; matrix products, arithmetic and copies ran while one was open for 1% -> 0% of each run, Pallas kernels for 0% -> 0%
where the time goes in v1:
time: 1160 us
  waiting for transfers between devices  830 us (72%)
  blocking collectives  291 us (25%)
  between operations  14.1 us (1%)
    unnamed x5, waiting for transfers between devices  749 us
    psum x1, blocking collectives, local(): lax.psum(lax.psum((sums[0], sums[1], sums[2], sums[3]), 'dp'), 'grid')  108 us
    psum x1, waiting for transfers between devices, local(): lax.psum((sums[0], sums[1], sums[2], sums[3]), 'dp')  80.8 us
    all_gather x1, blocking collectives, local(): piece = lax.all_gather(grad_in, 'grid', axis=0, tiled=True)  68.3 us
    all_gather x1, blocking collectives, local(): piece = lax.all_gather(mixed, 'grid', axis=0, tiled=True)  61 us
    psum x1, blocking collectives, local(): lax.psum(spectral_part.astype(jnp.bfloat16), 'dp').astype(jnp.float32)  34.5 us
  transfers between devices with their start and end apart: 3, of which 3 were waited for; matrix products, arithmetic and copies ran while one was open for 0% of the time, Pallas kernels for 0%

profile of v1, /device:TPU:1, one launch (start us, length us, event | category | flops | bytes accessed | tf_op | source)
XLA Modules:
  0.0 1160.3 jit_solution(15053911949582868023)
XLA Ops:
  7.3 0.7 broadcast_multiply_fusion.4
  8.0 0.1 iota_add_fusion.1
  8.0 0.1 add.115
  8.1 1.2 cosine_multiply_fusion
  9.4 0.1 multiply_convert_fusion.1
  9.4 0.3 copy.27
  9.7 0.1 convert_element_type.146
  9.8 0.2 fusion.47
  10.0 0.6 reshape.368
  10.8 0.2 reshape.377
  11.0 0.3 convert_reduce_fusion.1
  11.3 0.2 reshape.384
  11.5 0.3 copy.26
  11.8 0.1 convert_element_type.145
  11.9 0.3 copy.28
  12.2 1.3 dynamic-slice
  13.5 363.8 %all-reduce.10.cloned.1.call-done = f32[64,256]{1,0:T(8,128)} async-done(((f32[64,256]{1,0:T(8,128)}), f32[64,256]{1,0:T(8,128)}) %all-reduce.10.cloned.1.call-update) | async-done | bytes 65552
  377.3 1.4 dynamic-slice_reduce_fusion.1
  378.7 0.1 reshape.369
  378.8 0.1 fusion.27
  378.9 0.1 fusion.35
  379.0 0.1 fusion.20
  379.1 0.1 fusion.21
  379.3 0.1 reshape.385
  379.4 61.0 %all-gather = bf16[64,1,256]{2,1,0:T(2,128)(2,1)S(1)} all-gather(bf16[1,1,256]{2,1,0:T(2,128)(2,1)S(1)} %reshape.385), channel_id=1, replica_groups=mesh['grid'=64,'dp'=8] {'grid'}, dimensions={0}, use_global_device_ids=true | all-gather | bytes 33280 | tf_op jit(solution)/shard_map/all_gather | solution.py:113
  440.3 0.2 reduce.1
  440.5 0.3 convolution_convert_fusion.1
  440.8 0.2 reshape.375
  441.1 0.9 multiply_convert_fusion
  442.0 1.5 convert_reduce_fusion
  443.5 0.9 fusion.49
  444.4 0.4 convolution_convert_fusion
  444.8 0.9 fusion.50
  445.8 0.3 copy.30
  446.1 0.3 reshape.378
  446.3 0.2 fusion.48
  446.5 0.6 reshape.379
  447.2 0.4 fusion.2
  447.6 0.3 copy.29
  447.9 1.0 reshape.376
  448.9 19.3 %all-reduce.4 = (f32[256]{0:T(256)S(1)}, f32[64]{0:T(128)S(1)}) all-reduce(f32[256]{0:T(256)S(1)} %get-tuple-element.22, f32[64]{0:T(128)S(1)} %convert_reduce_fusion.1), channel_id=1, replica_groups=mesh['grid'=64,'dp'=8] {'dp'}, use_global_device_ids=true, to_apply=%region_6.7 | all-reduce | flops 320 | bytes 2560 | tf_op jit(solution)/shard_map/psum | solution.py:143
  468.2 108.0 %all-reduce.2 = (f32[256]{0:T(256)S(1)}, f32[64]{0:T(128)S(1)}) all-reduce(f32[256]{0:T(256)S(1)} %get-tuple-element.12, f32[64]{0:T(128)S(1)} %get-tuple-element.13), channel_id=1, replica_groups=mesh['grid'=64,'dp'=8] {'grid'}, use_global_device_ids=true, to_apply=%region_7.8 | all-reduce | flops 320 | bytes 2560 | tf_op jit(solution)/shard_map/psum | solution.py:142
  576.2 0.6 broadcast_multiply_fusion.2
  576.8 80.8 %all-reduce.14.cloned.1.call-done = (f32[64,256]{1,0:T(8,128)}, f32[256,64]{0,1:T(8,128)}) async-done(((f32[64,256]{1,0:T(8,128)}, f32[256,64]{0,1:T(8,128)}), (f32[64,256]{1,0:T(8,128)}, f32[256,64]{0,1:T(8,128)})) %all-reduce.14.cloned.1.call-update) | async-done | bytes 131088 | tf_op jit(solution)/shard_map/psum | solution.py:143
  657.7 0.5 broadcast_multiply_fusion.3
  658.2 384.9 %all-reduce.12.cloned.1.call-done = (f32[64,256]{1,0:T(8,128)}, f32[64,256]{1,0:T(8,128)}, f32[256,64]{0,1:T(8,128)}) async-done(((f32[64,256]{1,0:T(8,128)}, f32[64,256]{1,0:T(8,128)}, f32[256,64]{0,1:T(8,128)}), (f32[64,256]{1,0:T(8,128)}, f32[64,256]{1,0:T(8,128)}, f32[256,64]{0,1:T(8,128)})) %all-reduce.12.cloned.1.call-update) | async-done | bytes 196624
  1043.1 1.4 dynamic-slice_reduce_fusion
  1044.5 0.1 reshape.380
  1044.5 0.2 fusion.46
  1044.8 0.2 fusion.45
  1045.0 0.1 fusion.32
  1045.1 0.1 fusion.30
  1045.3 0.3 fusion.13
  1045.6 0.2 fusion.12
  1045.8 34.5 %psum.63 = bf16[2,1,64,64]{3,2,1,0:T(8,128)(2,1)S(1)} all-reduce(bf16[2,1,64,64]{3,2,1,0:T(8,128)(2,1)S(1)} %pad_maximum_fusion), channel_id=1, replica_groups=mesh['grid'=64,'dp'=8] {'dp'}, use_global_device_ids=true, to_apply=%region_2.3 | all-reduce | flops 8192 | bytes 32768 | tf_op jit(solution)/shard_map/psum | solution.py:141
  1080.3 0.6 convert_multiply_fusion
  1081.0 0.1 fusion.19
  1081.1 0.1 fusion.18
  1081.3 0.1 reshape.387
  1081.4 68.3 %all-gather.1 = bf16[64,1,256]{2,1,0:T(2,128)(2,1)S(1)} all-gather(bf16[1,1,256]{2,1,0:T(2,128)(2,1)S(1)} %reshape.387), channel_id=1, replica_groups=mesh['grid'=64,'dp'=8] {'grid'}, dimensions={0}, use_global_device_ids=true | all-gather | bytes 33280 | tf_op jit(solution)/shard_map/all_gather | solution.py:133
  1149.7 0.2 reduce.3
  1149.9 1.0 fusion.9
  1150.9 1.5 broadcast_multiply_fusion
  1152.3 1.5 broadcast_multiply_fusion.1
  (26 shorter events, 0.3 us)
Async XLA Ops:
  7.2 433.9 %copy-start = (bf16[64,256]{1,0:T(8,128)(2,1)S(1)}, bf16[64,256]{1,0:T(8,128)(2,1)}, u32[]{:S(2)}) copy-start(bf16[64,256]{1,0:T(8,128)(2,1)} %param.12) | copy-start | bytes 98308
  7.2 2.6 copy-start.2
  7.2 3.6 copy-start.1
  7.2 370.1 %all-reduce.10.cloned.1.call-start = ((), (), s32[]{:S(2)}) async-start(), calls=%async_computation | async-start | bytes 131072
  10.7 646.9 %all-reduce.14.cloned.1.call-start = ((), (), s32[]{:S(2)}) async-start(), calls=%async_computation.2 | async-start | bytes 262144 | tf_op jit(solution)/shard_map/psum | solution.py:143
  11.3 367.4 %copy-start.3 = (bf16[2,1,64,64]{3,2,1,0:T(8,128)(2,1)S(1)}, bf16[2,1,64,64]{3,2,1,0:T(8,128)(2,1)}, u32[]{:S(2)}) copy-start(bf16[2,1,64,64]{3,2,1,0:T(8,128)(2,1)} %param.11) | copy-start | bytes 49156
  11.5 429.6 %copy-start.6 = (f32[256]{0:T(256)S(1)}, f32[256]{0:T(256)}, u32[]{:S(2)}) copy-start(f32[256]{0:T(256)} %param.13) | copy-start | bytes 3076
  441.1 0.9 copy-start.4
  444.8 2.4 copy-start.5
  576.2 466.9 %all-reduce.12.cloned.1.call-start = ((), (), s32[]{:S(2)}) async-start(), calls=%async_computation.1 | async-start | bytes 393216
Sparse Core Ops, SparseCore 0:
  11.5 365.7 all-reduce.9
  576.3 81.2 all-reduce.13
  661.3 381.7 all-reduce.11
